TPU v7x, 32 devices: a whole 2x2x4 slice. The times are simulated.
32 devices in a mesh: row: 4 (over z), col: 8 (over y, x, core).
Axes of the slice: x: 2, y: 2, z: 4, core: 2. Of those that a mesh axis runs over, the one named last changes fastest.
Arguments:
- spectra: bfloat16 [1024, 32, 128], P(('row', 'col')), may hold values from -6 to 6
- pair_bins: int32 [1024, 1024], P('row', 'col'), may hold values from 0 to 255
- row_subs: int32 [4, 16], P('row'), may hold values from 0 to 31, as said below
- station_subs: int32 [1024, 8], replicated, may hold values from 0 to 31, as said below
- kernel: bfloat16 [32, 256, 256], replicated, may hold values from -0.375 to 0.375
Outputs:
- spectrum: float32 [32, 32, 256], P(('row', 'col'))
Inputs may be any that keep to these rules, and one draw needn't show every extreme that they name: `row_subs`: each row lists 16 distinct subarrays; each subarray is listed for exactly two row blocks. `station_subs`: each station names 8 distinct subarrays, all listed in row_subs for the station's row block.
All inputs are finite; a program needn't handle non-finite values.
Results may differ from a plain program's by a relative error of at most 0.0039.
Values may be sent and summed in bfloat16 or wider, within the bound.
A program may use at most 64 MiB of HBM per device.

v0:
```python
import math

import jax
import jax.numpy as jnp
from jax import lax
from jax.sharding import PartitionSpec as P

F = 32
NBIN = 256
SUB_DEV = 1


def spread_rows(slot_terms, slot_subs, row_count):
    targets = jnp.arange(row_count, dtype=jnp.int32)
    selector = (targets[:, None] == slot_subs[None, :]).astype(jnp.float32)
    return jnp.dot(selector, slot_terms, precision=lax.Precision.HIGHEST)


def project(owned_bins, kernel):
    velocity_power = jnp.einsum(
        "sfb,fbv->sfv", owned_bins, kernel, preferred_element_type=jnp.float32
    )
    scale = lax.rsqrt(jnp.mean(velocity_power * velocity_power, axis=2, keepdims=True) + 1e-06)
    return velocity_power * scale


def on_device(spectra, pair_bins, row_subs, station_subs, kernel):
    shard_rows = spectra.shape[0]
    col_total = lax.axis_size("col")
    row_index = lax.axis_index("row")
    col_index = lax.axis_index("col")
    row_spectra = lax.all_gather(spectra, "col", axis=0, tiled=True)
    col_spectra = lax.all_gather(spectra, "row", axis=0, tiled=True)
    row_span = row_spectra.shape[0]
    col_span = col_spectra.shape[0]
    slot_subs = row_subs[0]
    slot_count = slot_subs.shape[0]
    row_members = lax.dynamic_slice_in_dim(station_subs, row_index * row_span, row_span, 0)
    positions = jnp.arange(col_span, dtype=jnp.int32)
    col_ids = (
        positions // shard_rows * col_total + col_index
    ) * shard_rows + positions % shard_rows
    col_members = jnp.take(station_subs, col_ids, axis=0)
    row_mask = jnp.any(row_members[None, :, :] == slot_subs[:, None, None], axis=2).astype(
        jnp.bfloat16
    )
    col_mask = jnp.any(col_members[None, :, :] == slot_subs[:, None, None], axis=2).astype(
        jnp.bfloat16
    )
    cross_spec = jnp.einsum(
        "aft,jft->faj", row_spectra, col_spectra, preferred_element_type=jnp.float32
    ).astype(jnp.bfloat16)
    step_rows = math.gcd(row_span, max(1, 2048 // col_span))
    step_count = row_span // step_rows
    bin_ids = jnp.arange(NBIN, dtype=jnp.int32)

    def accumulate(step_index, running):
        first_row = step_index * step_rows
        cross_part = lax.dynamic_slice_in_dim(cross_spec, first_row, step_rows, 1)
        mask_part = lax.dynamic_slice_in_dim(row_mask, first_row, step_rows, 1)
        bins_part = lax.dynamic_slice_in_dim(pair_bins, first_row, step_rows, 0)
        weighted = mask_part[:, None, :, None] * col_mask[:, None, None, :] * cross_part[None]
        onehot = (bins_part.reshape(-1, 1) == bin_ids[None, :]).astype(jnp.bfloat16)
        return running + jnp.dot(
            weighted.reshape(slot_count * F, step_rows * col_span),
            onehot,
            preferred_element_type=jnp.float32,
        )

    partial_value = lax.fori_loop(
        0, step_count, accumulate, jnp.zeros((slot_count * F, NBIN), jnp.float32)
    )
    partial_value = partial_value.reshape(slot_count, F, NBIN)
    freq_part = lax.psum_scatter(partial_value, "col", scatter_dimension=1, tiled=True)
    freq_share = freq_part.shape[1]
    group_rows = SUB_DEV * col_total
    summed = lax.psum_scatter(
        spread_rows(
            freq_part.reshape(slot_count, freq_share * NBIN),
            slot_subs,
            lax.axis_size("row") * group_rows,
        ),
        "row",
        scatter_dimension=0,
        tiled=True,
    )
    binned = summed.reshape(group_rows, freq_share, NBIN).astype(jnp.bfloat16)
    return project(lax.all_to_all(binned, "col", split_axis=0, concat_axis=1, tiled=True), kernel)


def solution(mesh):
    in_specs = (P(("row", "col"), None, None), P("row", "col"), P("row", None), P(), P())
    out_specs = P(("row", "col"), None, None)
    return jax.shard_map(
        on_device, mesh=mesh, in_specs=in_specs, out_specs=out_specs, check_vma=False
    )
```

profile of v0, /device:TPU:0, one launch (start us, length us, event | category | flops | bytes accessed | tf_op | source)
XLA Modules:
  0.0 180.9 jit_solution(14719300169441912463)
XLA Ops:
  6.5 1.8 copy.29
  8.4 0.7 all-gather.3.cloned.1.call-update
  9.2 1.0 copy.27
  10.1 0.7 constant_dynamic-slice_fusion.2
  10.8 0.8 compare_reduce_fusion
  11.7 0.6 gather_fusion
  12.6 27.1 %all-gather.5.cloned.1.call-done = bf16[128,32,128]{2,0,1:T(8,128)(2,1)} async-done(((bf16[32,32,128]{2,0,1:T(8,128)(2,1)}), bf16[128,32,128]{2,0,1:T(8,128)(2,1)}) %all-gather.5.cloned.1.call-update) | async-done | bytes 1048592 | tf_op jit(solution)/shard_map/all_gather | solution.py:33
  39.6 29.4 %all-gather.3.cloned.1.call-done = bf16[256,32,128]{2,0,1:T(8,128)(2,1)} async-done(((bf16[32,32,128]{2,0,1:T(8,128)(2,1)}), bf16[256,32,128]{2,0,1:T(8,128)(2,1)}) %all-gather.3.cloned.1.call-update) | async-done | bytes 2097168 | tf_op jit(solution)/shard_map/all_gather | solution.py:32
  69.0 2.6 %convolution_convert_fusion = bf16[32,256,128]{2,1,0:T(8,128)(2,1)S(1)} fusion(bf16[256,32,128]{2,0,1:T(8,128)(2,1)} %all-gather.3.cloned.1.call-done, bf16[128,32,128]{2,0,1:T(8,128)(2,1)} %all-gather.5.cloned.1.call-done), kind=kOutput, calls=%fused_computation.13 | convolution fusion | flops 269484032 | bytes 5242880 | tf_op jit(solution)/shard_map/aft,jft->faj/dot_general | solution.py:50
  71.6 33.1 %while.14 = (s32[]{:T(128)}, f32[512,256]{1,0:T(8,128)S(1)}, bf16[16,256]{1,0:T(8,128)(2,1)S(1)}, bf16[16,128]{1,0:T(8,128)(2,1)S(1)}, bf16[32,256,128]{2,1,0:T(...) while((s32[]{:T(128)}, f32[512,256]{1,0:T(8,128)S(1)}, ...), condition=%wide.region_3.4_spmd.clone, body=%wide.region_2.3_spmd.clone.sunk | while | flops 538738688 | bytes 5797553 | solution.py:70
  71.7 0.7 dynamic-slice_bitcast_fusion.2
  72.5 0.1 broadcast_multiply_fusion.5
  72.7 1.0 fusion.31
  73.8 0.7 dynamic-slice_bitcast_fusion.2
  74.6 0.1 broadcast_multiply_fusion.5
  74.8 1.0 fusion.31
  75.8 0.7 dynamic-slice_bitcast_fusion.2
  76.7 0.1 broadcast_multiply_fusion.5
  76.8 1.0 fusion.31
  77.9 0.7 dynamic-slice_bitcast_fusion.2
  78.8 0.1 broadcast_multiply_fusion.5
  78.9 1.0 fusion.31
  80.0 0.7 dynamic-slice_bitcast_fusion.2
  80.8 0.1 broadcast_multiply_fusion.5
  81.0 1.0 fusion.31
  82.1 0.7 dynamic-slice_bitcast_fusion.2
  82.9 0.1 broadcast_multiply_fusion.5
  83.0 1.0 fusion.31
  84.1 0.7 dynamic-slice_bitcast_fusion.2
  85.0 0.1 broadcast_multiply_fusion.5
  85.1 1.0 fusion.31
  86.2 0.7 dynamic-slice_bitcast_fusion.2
  87.0 0.1 broadcast_multiply_fusion.5
  87.2 1.0 fusion.31
  88.3 0.7 dynamic-slice_bitcast_fusion.2
  89.1 0.1 broadcast_multiply_fusion.5
  89.3 1.0 fusion.31
  90.3 0.7 dynamic-slice_bitcast_fusion.2
  91.2 0.1 broadcast_multiply_fusion.5
  91.3 1.0 fusion.31
  92.4 0.7 dynamic-slice_bitcast_fusion.2
  93.3 0.1 broadcast_multiply_fusion.5
  93.4 1.0 fusion.31
  94.5 0.7 dynamic-slice_bitcast_fusion.2
  95.3 0.1 broadcast_multiply_fusion.5
  95.5 1.0 fusion.31
  96.6 0.7 dynamic-slice_bitcast_fusion.2
  97.4 0.1 broadcast_multiply_fusion.5
  97.5 1.0 fusion.31
  98.6 0.7 dynamic-slice_bitcast_fusion.2
  99.6 1.0 fusion.31
  100.7 0.7 dynamic-slice_bitcast_fusion.2
  101.7 1.0 fusion.31
  102.8 0.7 dynamic-slice_bitcast_fusion.2
  103.8 1.0 fusion.31
  104.8 1.1 copy.31
  105.9 34.2 %reduce-scatter.3.cloned.1.call-done = f32[16,4,256]{2,0,1:T(8,128)} async-done(((f32[16,32,256]{2,0,1:T(8,128)}), f32[16,4,256]{2,0,1:T(8,128)}) %reduce-scatter.3.cloned.1.call-update) | async-done | bytes 65552 | tf_op jit(solution)/shard_map/reduce_scatter | solution.py:74
  140.2 0.8 copy.37
  141.0 0.8 fusion.11
  141.9 19.9 %reduce-scatter.5.cloned.1.call-done = f32[8,1024]{1,0:T(8,128)} async-done(((f32[32,1024]{1,0:T(8,128)}), f32[8,1024]{1,0:T(8,128)}) %reduce-scatter.5.cloned.1.call-update) | async-done | bytes 32784 | tf_op jit(solution)/shard_map/reduce_scatter | solution.py:77
  161.7 0.8 convert_element_type.22
  162.5 8.2 %all_to_all.4 = bf16[8,4,256]{2,1,0:T(4,128)(2,1)S(1)} all-to-all(bf16[8,4,256]{2,1,0:T(4,128)(2,1)S(1)} %copy.33), channel_id=1, replica_groups=mesh['row'=4,'col'=8] {'col'}, dimensions={0} | all-to-all | bytes 32768 | tf_op jit(solution)/shard_map/all_to_all | solution.py:88
  170.7 2.8 %fusion.22 = f32[32,1,256]{2,1,0:T(1,128)S(1)} fusion(bf16[32,256,1]{1,2,0:T(2,128)(2,1)S(1)} %reshape.159, bf16[32,256,256]{2,1,0:T(8,128)(2,1)} %param.11), kind=kOutput, calls=%fused_computation.49 | convolution fusion | flops 4194304 | bytes 4243456 | tf_op jit(solution)/shard_map/sfb,fbv->sfv/dot_general | solution.py:20
  173.7 0.7 fusion.10
  (73 shorter events, 4.3 us)
Async XLA Ops:
  6.5 5.9 %copy-start = (s32[1,16]{1,0:T(1,128)S(1)}, s32[1,16]{1,0:T(1,128)}, u32[]{:S(2)}) copy-start(s32[1,16]{1,0:T(1,128)} %param.9) | copy-start | bytes 196
  6.5 33.1 %all-gather.5.cloned.1.call-start = ((), (), s32[]{:S(2)}) async-start(), calls=%async_computation.4 | async-start | bytes 1310720 | tf_op jit(solution)/shard_map/all_gather | solution.py:33
  8.3 60.7 %all-gather.3.cloned.1.call-start = ((), (), s32[]{:S(2)}) async-start(), calls=%async_computation.3 | async-start | bytes 2359296 | tf_op jit(solution)/shard_map/all_gather | solution.py:32
  9.1 131.1 %reduce-scatter.3.cloned.1.call-start = ((), (), s32[]{:S(2)}) async-start(), calls=%async_computation.5 | async-start | bytes 589824 | tf_op jit(solution)/shard_map/reduce_scatter | solution.py:74
  105.9 55.8 %reduce-scatter.5.cloned.1.call-start = ((), (), s32[]{:S(2)}) async-start(), calls=%async_computation.6 | async-start | bytes 163840 | tf_op jit(solution)/shard_map/reduce_scatter | solution.py:77
Sparse Core Ops, SparseCore 0:
  8.9 30.6 all-gather.4
  41.5 27.4 all-gather.2
  106.0 34.1 reduce-scatter.2
  142.3 19.4 reduce-scatter.4
where the time goes:
time: 182 us; the launch traced here: 181 us
  waiting for transfers between devices  111 us (61%)
  matrix products  21.9 us (12%)
  local copies, waits for them, and re-layouts  19 us (10%)
  between operations  13.2 us (7%)
  blocking collectives  8.21 us (5%)
  other arithmetic  6.36 us (3%)
    reduce_scatter x1, waiting for transfers between devices, on_device(): lax.psum_scatter(partial_value, 'col', scatter_dimension=1, tiled=True)  34.2 us
    all_gather x1, waiting for transfers between devices, on_device(): row_spectra = lax.all_gather(spectra, 'col', axis=0, tiled=True)  29.4 us
    all_gather x1, waiting for transfers between devices, on_device(): col_spectra = lax.all_gather(spectra, 'row', axis=0, tiled=True)  27.1 us
    reduce_scatter x1, waiting for transfers between devices, on_device(): lax.psum_scatter(spread_rows(freq_part.reshape(slot_count, freq_share * N...  19.9 us
    dot_general x16, matrix products, accumulate(): jnp.dot(weighted.reshape(slot_count * F, step_rows * col_span), onehot, p...  15.6 us
    eq x16, local copies, waits for them, and re-layouts, accumulate(): onehot = (bins_part.reshape(-1, 1) == bin_ids[None, :]).astype(jnp.bfloat16)  11.2 us
    all_to_all x1, blocking collectives, on_device(): lax.all_to_all(binned, 'col', split_axis=0, concat_axis=1, tiled=True)  8.21 us
    mul x32, other arithmetic, accumulate(): mask_part[:, None, :, None] * col_mask[:, None, None, :] * cross_part[None]  3.76 us
  transfers between devices with their start and end apart: 4, of which 4 were waited for; matrix products, arithmetic and copies ran while one was open for 2% of the time, Pallas kernels for 0%

commit v1 on v0

v1 whole, which is shorter than its diff:
```python
import functools

import jax
import jax.numpy as jnp
from jax import lax
from jax.experimental import pallas as pl
from jax.experimental.pallas import tpu as pltpu
from jax.sharding import PartitionSpec as P

MESH = pl.DeviceIdType.MESH
NT = (((1,), (1,)), ((), ()))
NBIN = 256
PIECES = 4
UNROLL = 8


def gather_kernel(x_ref, row_ref, col_ref, own_sem, row_send, row_recv, sib_send, sib_recv,
                  fwd_send, fwd_recv, col_send, col_recv):
    rows, cols = lax.axis_size("row"), lax.axis_size("col")
    r, c = lax.axis_index("row"), lax.axis_index("col")
    freqs, shard = x_ref.shape[0], x_ref.shape[1]
    pairs = cols // 2
    g, h = c // 2, c % 2
    sib = g * 2 + (1 - h)
    span = freqs // PIECES

    barrier = pltpu.get_barrier_semaphore()
    for d in range(1, pairs):
        pl.semaphore_signal(barrier, inc=1, device_id=(r, lax.rem(g + d, pairs) * 2 + h), device_id_type=MESH)
    pl.semaphore_signal(barrier, inc=1, device_id=(r, sib), device_id_type=MESH)
    for d in range(1, rows):
        pl.semaphore_signal(barrier, inc=1, device_id=(lax.rem(r + d, rows), c), device_id_type=MESH)

    def slot(ref, index, piece):
        return ref.at[pl.ds(piece * span, span), pl.ds(pl.multiple_of(index * shard, shard), shard), :]

    own_row = pltpu.make_async_copy(x_ref, row_ref.at[:, pl.ds(pl.multiple_of(c * shard, shard), shard), :], own_sem.at[0])
    own_col = pltpu.make_async_copy(x_ref, col_ref.at[:, pl.ds(pl.multiple_of(r * shard, shard), shard), :], own_sem.at[1])
    own_row.start()
    own_col.start()
    pl.semaphore_wait(barrier, pairs - 1 + 1 + rows - 1)

    started = []
    row_copies = {}
    for k in range(PIECES):
        piece = x_ref.at[pl.ds(k * span, span)]
        for d in range(1, rows):
            copy = pltpu.make_async_remote_copy(
                piece, slot(col_ref, r, k), col_send.at[d, k], col_recv.at[d, k],
                device_id=(lax.rem(r + d, rows), c), device_id_type=MESH)
            copy.start()
            started.append(copy)
        for d in range(1, pairs):
            copy = pltpu.make_async_remote_copy(
                piece, slot(row_ref, c, k), row_send.at[d, k], row_recv.at[d, k],
                device_id=(r, lax.rem(g + d, pairs) * 2 + h), device_id_type=MESH)
            copy.start()
            row_copies[d, k] = copy
        copy = pltpu.make_async_remote_copy(
            piece, slot(row_ref, c, k), sib_send.at[k], sib_recv.at[k],
            device_id=(r, sib), device_id_type=MESH)
        copy.start()
        started.append(copy)
    for k in range(PIECES):
        for d in range(1, pairs):
            row_copies[d, k].wait_recv()
            source = lax.rem(g - d + pairs, pairs) * 2 + h
            copy = pltpu.make_async_remote_copy(
                slot(row_ref, source, k), slot(row_ref, source, k), fwd_send.at[d, k], fwd_recv.at[d, k],
                device_id=(r, sib), device_id_type=MESH)
            copy.start()
            started.append(copy)
    for copy in row_copies.values():
        copy.wait_send()
    for copy in started:
        copy.wait()
    own_row.wait()
    own_col.wait()


def gather(x):
    rows, cols = lax.axis_size("row"), lax.axis_size("col")
    freqs, shard, width = x.shape
    pairs = cols // 2
    dma = pltpu.SemaphoreType.DMA
    return pl.pallas_call(
        gather_kernel,
        out_shape=(jax.ShapeDtypeStruct((freqs, cols * shard, width), x.dtype),
                   jax.ShapeDtypeStruct((freqs, rows * shard, width), x.dtype)),
        in_specs=[pl.BlockSpec(memory_space=pl.ANY)],
        out_specs=(pl.BlockSpec(memory_space=pl.ANY),) * 2,
        scratch_shapes=[dma((2,)), dma((pairs, PIECES)), dma((pairs, PIECES)), dma((PIECES,)), dma((PIECES,)),
                        dma((pairs, PIECES)), dma((pairs, PIECES)), dma((rows, PIECES)), dma((rows, PIECES))],
        compiler_params=pltpu.CompilerParams(collective_id=0, has_side_effects=True),
        name="gather_spectra",
    )(x)


def bin_kernel(cols, row_ref, col_ref, bins_ref, rmask_ref, cmask_ref, out_ref, cross, w0, o0, w1, o1, acc):
    freqs, span, _ = row_ref.shape
    width = col_ref.shape[1]
    slots = cmask_ref.shape[0]

    def one_freq(f, carry):
        cross[pl.ds(f, span, stride=freqs), :] = lax.dot_general(
            row_ref[f], col_ref[f], NT, preferred_element_type=jnp.float32)
        return carry

    lax.fori_loop(0, freqs, one_freq, 0, unroll=4)
    steps = span // UNROLL

    def build(step, w, o):
        for u in range(UNROLL):
            i = step * UNROLL + u
            block = cross[pl.ds(pl.multiple_of(i * freqs, freqs), freqs), :].astype(jnp.bfloat16)
            mask = rmask_ref[i] * cmask_ref[...]
            weighted = mask[:, None, :] * block[None]
            w[:, u * width:(u + 1) * width] = weighted.reshape(slots * freqs, width)
            ids = lax.broadcasted_iota(jnp.int32, (NBIN, width), 0)
            o[:, u * width:(u + 1) * width] = jnp.where(ids == bins_ref[pl.ds(i, 1), :], 1.0, 0.0).astype(jnp.bfloat16)

    def multiply(w, o):
        acc[...] += lax.dot_general(w[...], o[...], NT, preferred_element_type=jnp.float32)

    acc[...] = jnp.zeros_like(acc)
    build(0, w0, o0)

    def two(pair, carry):
        build(2 * pair + 1, w1, o1)
        multiply(w0, o0)
        build(lax.min(2 * pair + 2, steps - 1), w0, o0)
        multiply(w1, o1)
        return carry

    lax.fori_loop(0, steps // 2, two, 0)
    share = freqs // cols
    for k in range(cols):
        for s in range(slots):
            out_ref[k, s * share:(s + 1) * share, :] = acc[s * freqs + k * share:s * freqs + (k + 1) * share, :]


def bin_pairs(row_spectra, col_spectra, pair_bins, row_mask, col_mask):
    cols = lax.axis_size("col")
    freqs, span, _ = row_spectra.shape
    width = col_spectra.shape[1]
    slots = col_mask.shape[0]
    vmem = pl.BlockSpec(memory_space=pltpu.VMEM)
    return pl.pallas_call(
        functools.partial(bin_kernel, cols),
        out_shape=jax.ShapeDtypeStruct((cols, slots * freqs // cols, NBIN), jnp.float32),
        in_specs=[vmem] * 5,
        out_specs=vmem,
        scratch_shapes=[
            pltpu.VMEM((span * freqs, width), jnp.float32),
            pltpu.VMEM((slots * freqs, UNROLL * width), jnp.bfloat16),
            pltpu.VMEM((NBIN, UNROLL * width), jnp.bfloat16),
            pltpu.VMEM((slots * freqs, UNROLL * width), jnp.bfloat16),
            pltpu.VMEM((NBIN, UNROLL * width), jnp.bfloat16),
            pltpu.VMEM((slots * freqs, NBIN), jnp.float32),
        ],
        name="bin_pairs",
    )(row_spectra, col_spectra, pair_bins, row_mask, col_mask)


def split(x, n):
    if n & (n - 1) == 0:
        return x >> (n.bit_length() - 1), x & (n - 1)
    return lax.div(x, n), lax.rem(x, n)


def finish_kernel(part_ref, subs_ref, kern_ref, out_ref, got1, spread, got2, ready, got3, kern,
                  kern_sem, send1, recv1, send2, recv2, send3, recv3):
    rows, cols = lax.axis_size("row"), lax.axis_size("col")
    r, c = lax.axis_index("row"), lax.axis_index("col")
    share = kern.shape[0]
    freqs = share * cols

    barrier = pltpu.get_barrier_semaphore()
    for d in range(1, cols):
        pl.semaphore_signal(barrier, inc=1, device_id=(r, lax.rem(c + d, cols)), device_id_type=MESH)
    for d in range(1, rows):
        pl.semaphore_signal(barrier, inc=1, device_id=(lax.rem(r + d, rows), c), device_id_type=MESH)
    fetch = pltpu.make_async_copy(kern_ref.at[pl.ds(c * share, share)], kern, kern_sem)
    fetch.start()
    pl.semaphore_wait(barrier, cols + rows - 2)

    copies = []
    for d in range(1, cols):
        to = lax.rem(c + d, cols)
        copy = pltpu.make_async_remote_copy(
            part_ref.at[to], got1.at[d], send1.at[d], recv1.at[d], device_id=(r, to), device_id_type=MESH)
        copy.start()
        copies.append(copy)
    depth = part_ref.shape[1]
    shape = (rows * freqs, depth)
    rid, rest = split(lax.broadcasted_iota(jnp.int32, shape, 0), freqs)
    fid, sid = split(rest, cols)
    _, fin = split(lax.broadcasted_iota(jnp.int32, shape, 1), share)
    chosen = jnp.where((rid * cols + sid == subs_ref[...]) & (fid == fin), 1.0, 0.0)
    total = part_ref[c]
    for d in range(1, cols):
        copies[d - 1].wait()
        total = total + got1[d]
    spread[...] = jnp.dot(chosen, total, precision=lax.Precision.HIGHEST,
                          preferred_element_type=jnp.float32).reshape(spread.shape)
    copies = []
    for d in range(1, rows):
        to = lax.rem(r + d, rows)
        copy = pltpu.make_async_remote_copy(
            spread.at[to], got2.at[d], send2.at[d], recv2.at[d], device_id=(to, c), device_id_type=MESH)
        copy.start()
        copies.append(copy)
    total = spread[r]
    fetch.wait()
    for d in range(1, rows):
        copies[d - 1].wait()
        total = total + got2[d]
    binned = total.astype(jnp.bfloat16)
    for f in range(share):
        power = jnp.dot(binned[f * cols:(f + 1) * cols], kern[f], preferred_element_type=jnp.float32)
        scale = lax.rsqrt(jnp.mean(power * power, axis=1, keepdims=True) + 1e-06)
        power = power * scale
        for k in range(cols):
            ready[k, f:f + 1, :] = power[k:k + 1]
    copies = []
    for d in range(1, cols):
        to = lax.rem(c + d, cols)
        copy = pltpu.make_async_remote_copy(
            ready.at[to], got3.at[d], send3.at[d], recv3.at[d], device_id=(r, to), device_id_type=MESH)
        copy.start()
        copies.append(copy)
    out_ref[c] = ready[c]
    for d in range(1, cols):
        copies[d - 1].wait()
        out_ref[lax.rem(c - d + cols, cols)] = got3[d]


def finish(partial_value, slot_subs, kernel):
    rows, cols = lax.axis_size("row"), lax.axis_size("col")
    depth = partial_value.shape[1]
    freqs, _, speeds = kernel.shape
    share = freqs // cols
    dma = pltpu.SemaphoreType.DMA
    vmem = pl.BlockSpec(memory_space=pltpu.VMEM)
    return pl.pallas_call(
        finish_kernel,
        out_shape=jax.ShapeDtypeStruct((cols, share, speeds), jnp.float32),
        in_specs=[vmem, vmem, pl.BlockSpec(memory_space=pl.ANY)],
        out_specs=vmem,
        scratch_shapes=[
            pltpu.VMEM((cols, depth, NBIN), jnp.float32),
            pltpu.VMEM((rows, freqs, NBIN), jnp.float32),
            pltpu.VMEM((rows, freqs, NBIN), jnp.float32),
            pltpu.VMEM((cols, share, speeds), jnp.float32),
            pltpu.VMEM((cols, share, speeds), jnp.float32),
            pltpu.VMEM((share, NBIN, speeds), jnp.bfloat16),
            dma, dma((cols,)), dma((cols,)), dma((rows,)), dma((rows,)), dma((cols,)), dma((cols,)),
        ],
        compiler_params=pltpu.CompilerParams(collective_id=1, has_side_effects=True),
        name="finish",
    )(partial_value, jnp.repeat(slot_subs, share)[None], kernel)


def on_device(spectra, pair_bins, row_subs, station_subs, kernel):
    shard, freqs, _ = spectra.shape
    rows, cols = lax.axis_size("row"), lax.axis_size("col")
    r, c = lax.axis_index("row"), lax.axis_index("col")
    row_spectra, col_spectra = gather(spectra.transpose(1, 0, 2))
    slot_subs = row_subs[0]
    slots = slot_subs.shape[0]
    members = station_subs.shape[1]
    row_members = lax.dynamic_slice_in_dim(station_subs, r * cols * shard, cols * shard, 0)
    col_members = lax.dynamic_index_in_dim(
        station_subs.reshape(rows, cols, shard, members), c, 1, keepdims=False).reshape(rows * shard, members)
    row_mask = jnp.any(row_members[:, None, :] == slot_subs[None, :, None], axis=2).astype(jnp.bfloat16)
    col_mask = jnp.any(col_members[None, :, :] == slot_subs[:, None, None], axis=2).astype(jnp.bfloat16)
    row_mask = jnp.broadcast_to(row_mask[:, :, None], (cols * shard, slots, rows * shard))
    partial_value = bin_pairs(row_spectra, col_spectra, pair_bins, row_mask, col_mask)
    return finish(partial_value, slot_subs, kernel).reshape(1, freqs, kernel.shape[2])


def solution(mesh):
    in_specs = (P(("row", "col"), None, None), P("row", "col"), P("row", None), P(), P())
    out_specs = P(("row", "col"), None, None)
    return jax.shard_map(
        on_device, mesh=mesh, in_specs=in_specs, out_specs=out_specs, check_vma=False
    )
```

time: 182 us -> 85.6 us (0.47)
  waiting for transfers between devices: 111 us -> 0 us
  Pallas kernels: 0 us -> 75.9 us
  matrix products: 21.9 us -> 0 us
  between operations: 13.2 us -> 0.05 us
  local copies, waits for them, and re-layouts: 19 us -> 7.18 us
  blocking collectives: 8.21 us -> 0 us
  other arithmetic: 6.36 us -> 2.13 us
    pallas_call x0 -> x3, Pallas kernels: none -> 75.9 us  [the longest x1 30 us: gather(): pl.pallas_call(gather_kernel, out_shape=(jax.ShapeDtypeStruct((freqs, col...]
    all_gather x2 -> x0, waiting for transfers between devices: 56.4 us -> none  [the longest x1 29.4 us: on_device(): row_spectra = lax.all_gather(spectra, 'col', axis=0, tiled=True)]
    reduce_scatter x2 -> x0, waiting for transfers between devices: 54.1 us -> none  [the longest x1 34.2 us: on_device(): lax.psum_scatter(partial_value, 'col', scatter_dimension=1, tiled=True)]
    dot_general x19 -> x0, matrix products: 21.9 us -> none  [the longest x16 15.6 us: accumulate(): jnp.dot(weighted.reshape(slot_count * F, step_rows * col_span), onehot, p...]
    eq x16 -> x1, local copies, waits for them, and re-layouts: 11.2 us -> 0.08 us  [on_device(): col_members[None, :, :] == slot_subs[:, None, None]]
    all_to_all x1 -> x0, blocking collectives: 8.21 us -> none  [on_device(): lax.all_to_all(binned, 'col', split_axis=0, concat_axis=1, tiled=True)]
    mul x33 -> x0, other arithmetic: 4.46 us -> none  [the longest x32 3.76 us: accumulate(): mask_part[:, None, :, None] * col_mask[:, None, None, :] * cross_part[None]]
  transfers between devices with their start and end apart: 4 -> 0, of which waited for: 4 -> 0; matrix products, arithmetic and copies ran while one was open for 2% -> 0% of each run, Pallas kernels for 0% -> 0%
where the time goes in v1:
time: 85.6 us; the launch traced here: 85.2 us
  Pallas kernels  75.9 us (89%)
  local copies, waits for them, and re-layouts  7.18 us (8%)
  other arithmetic  2.13 us (2%)
    pallas_call x1, Pallas kernels, gather(): pl.pallas_call(gather_kernel, out_shape=(jax.ShapeDtypeStruct((freqs, col...  30 us
    pallas_call x1, Pallas kernels, bin_pairs(): pl.pallas_call(functools.partial(bin_kernel, cols), out_shape=jax.ShapeDt...  26.1 us
    pallas_call x1, Pallas kernels, finish(): pl.pallas_call(finish_kernel, out_shape=jax.ShapeDtypeStruct((cols, share...  19.8 us
    unnamed x3, local copies, waits for them, and re-layouts  1.74 us

profile of v1, /device:TPU:0, one launch (start us, length us, event | category | flops | bytes accessed | tf_op | source)
XLA Modules:
  0.0 85.2 jit_solution(17257511947636237816)
XLA Ops:
  0.0 0.0 copy-start
  0.0 0.7 constant_dynamic-slice_fusion.1
  0.7 0.8 compare_reduce_fusion
  1.5 0.1 copy.13
  1.6 1.6 %broadcast_in_dim.4.rmask_ref = bf16[256,16,128]{2,1,0:T(8,128)(2,1)} broadcast(bf16[256,16]{1,0:T(8,128)(2,1)S(1)} %copy.13), dimensions={0,1} | broadcast | bytes 1056768 | tf_op jit(solution)/shard_map/broadcast_in_dim | solution.py:277
  3.2 0.8 reshape.14
  4.1 0.1 eq.34
  4.2 0.8 compare_reduce_fusion.1
  4.9 0.6 convert_element_type.11.cmask_ref
  5.5 1.7 %copy.17 = bf16[32,32,128]{2,0,1:T(8,128)(2,1)} copy(bf16[32,32,128]{2,1,0:T(8,128)(2,1)} %param.5) | data formatting | bytes 524288 | tf_op args[0]
  7.3 30.0 %gather_spectra.1 = (bf16[32,256,128]{2,1,0:T(8,128)(2,1)}, bf16[32,128,128]{2,1,0:T(8,128)(2,1)}) custom-call(bf16[32,32,128]{2,1,0:T(8,128)(2,1)} %bitcast.9), custom_call_target="tpu_custom_call" | custom-call | tf_op jit(solution)/shard_map/gather_spectra/pallas_call | solution.py:86
  37.3 26.1 %bin_pairs.1.part_ref = f32[8,64,256]{2,1,0:T(8,128)} custom-call(bf16[32,256,128]{2,1,0:T(8,128)(2,1)} %get-tuple-element.7.row_ref, bf16[32,128,128]{2,1,0:T(8,128)(2,1)} %get-tuple-element.8.col_ref, s32[256,128]{1,0:T(8,128)} %bins_ref.1, bf16[256,16,128]{2,1,0:T(8,128)(2,1)} %broadcast_in_dim.4.rmask_ref, bf16[16,128]{1,0:T(8,128)(2,1)} %convert_element_type.11.cmask_ref), custom_call_target="tpu_custom_call" | custom-call | tf_op jit(solution)/shard_map/bin_pairs/pallas_call | solution.py:148
  63.4 0.0 copy-done
  63.4 0.1 broadcast_in_dim.5
  63.4 0.6 broadcast_in_dim_reshape.4.subs_ref
  64.0 19.8 %finish.1 = f32[8,4,256]{2,1,0:T(4,128)} custom-call(f32[8,64,256]{2,1,0:T(8,128)} %bin_pairs.1.part_ref, s32[1,64]{1,0:T(1,128)} %broadcast_in_dim_reshape.4.subs_ref, bf16[32,256,256]{2,1,0:T(8,128)(2,1)} %kern_ref.1), custom_call_target="tpu_custom_call" | custom-call | tf_op jit(solution)/shard_map/finish/pallas_call | solution.py:245
  83.8 1.4 %reshape.15 = f32[1,32,256]{2,1,0:T(8,128)} reshape(f32[8,4,256]{2,1,0:T(4,128)} %finish.1) | data formatting | bytes 65536 | tf_op jit(solution)/shard_map/reshape | solution.py:279
  (2 shorter events, 0.0 us)
Async XLA Ops:
  0.0 63.4 %copy-start = (s32[1,16]{1,0:T(1,128)S(1)}, s32[1,16]{1,0:T(1,128)}, u32[]{:S(2)}) copy-start(s32[1,16]{1,0:T(1,128)} %param.7) | copy-start | bytes 196

commit v2 on v0

v2 whole, which is shorter than its diff:
```python
import functools

import jax
import jax.numpy as jnp
from jax import lax
from jax.experimental import pallas as pl
from jax.experimental.pallas import tpu as pltpu
from jax.sharding import PartitionSpec as P

MESH = pl.DeviceIdType.MESH
NT = (((1,), (1,)), ((), ()))
NBIN = 256
HALVES = 2
PIECES = 4
UNROLL = 8
DIRECT = 2


def split(x, n):
    if n & (n - 1) == 0:
        return x >> (n.bit_length() - 1), x & (n - 1)
    return lax.div(x, n), lax.rem(x, n)


def body(rows, cols, x_ref, bins_ref, subs_ref, members_ref, kern_ref, out_ref,
         xf, xt, rowbuf, colbuf, member, pmask, onehot, cross, w0, w1, acc,
         part, got1, spread, got2, ready, got3, kern,
         own_sem, kern_sem, row_send, row_recv, sib_send, sib_recv, fwd_send, fwd_recv,
         col_send, col_recv, send1, recv1, send2, recv2, send3, recv3):
    r, c = lax.axis_index("row"), lax.axis_index("col")
    shard, freqs, _ = x_ref.shape
    span, width = bins_ref.shape
    slots = subs_ref.shape[1]
    pairs = cols // 2
    g, h = c // 2, c % 2
    sib = g * 2 + (1 - h)
    psize = freqs // PIECES
    half = freqs // HALVES
    share = half // cols
    steps = span // UNROLL
    bf16, f32 = jnp.bfloat16, jnp.float32

    barrier = pltpu.get_barrier_semaphore()
    for d in range(1, cols):
        pl.semaphore_signal(barrier, inc=1, device_id=(r, lax.rem(c + d, cols)), device_id_type=MESH)
    for d in range(1, rows):
        pl.semaphore_signal(barrier, inc=1, device_id=(lax.rem(r + d, rows), c), device_id_type=MESH)
    fetches = []
    for q in range(HALVES):
        fetch = pltpu.make_async_copy(kern_ref.at[pl.ds(q * half + c * share, share)], kern.at[q], kern_sem.at[q])
        fetch.start()
        fetches.append(fetch)
    xf[...] = x_ref[...].astype(f32).reshape(shard * freqs, x_ref.shape[2])
    for f in range(freqs):
        xt[f] = xf[pl.ds(f, shard, stride=freqs), :].astype(bf16)
    pl.semaphore_wait(barrier, cols + rows - 2)

    def slot(ref, index, k):
        return ref.at[pl.ds(k * psize, psize), pl.ds(pl.multiple_of(index * shard, shard), shard), :]

    def row_copy(d, k):
        return pltpu.make_async_remote_copy(
            xt.at[pl.ds(k * psize, psize)], slot(rowbuf, c, k), row_send.at[d, k], row_recv.at[d, k],
            device_id=(r, lax.rem(g + d, pairs) * 2 + h), device_id_type=MESH)

    def sib_copy(k):
        return pltpu.make_async_remote_copy(
            xt.at[pl.ds(k * psize, psize)], slot(rowbuf, c, k), sib_send.at[k], sib_recv.at[k],
            device_id=(r, sib), device_id_type=MESH)

    def fwd_copy(d, k):
        place = slot(rowbuf, lax.rem(g - d + pairs, pairs) * 2 + h, k)
        return pltpu.make_async_remote_copy(
            place, place, fwd_send.at[d, k], fwd_recv.at[d, k], device_id=(r, sib), device_id_type=MESH)

    def col_send_copy(way, d, k):
        if d <= DIRECT:
            return (r + way * d >= 0) & (r + way * d < rows), pltpu.make_async_remote_copy(
                xt.at[pl.ds(k * psize, psize)], slot(colbuf, r, k),
                col_send.at[(way + 1) // 2, d, k], col_recv.at[(way + 1) // 2, d, k],
                device_id=(lax.rem(r + way * d + rows, rows), c), device_id_type=MESH)
        source = lax.rem(r - way * (d - 1) + rows, rows)
        place = slot(colbuf, source, k)
        there = r + way
        back = r - way * (d - 1)
        return (there >= 0) & (there < rows) & (back >= 0) & (back < rows), pltpu.make_async_remote_copy(
            place, place, col_send.at[(way + 1) // 2, d, k], col_recv.at[(way + 1) // 2, d, k],
            device_id=(lax.rem(there + rows, rows), c), device_id_type=MESH)

    def col_wait(way, d, k):
        back = r - way * d

        @pl.when((back >= 0) & (back < rows))
        def _():
            place = slot(colbuf, lax.rem(back + rows, rows), k)
            pltpu.make_async_remote_copy(
                place, place, col_send.at[(way + 1) // 2, d, k], col_recv.at[(way + 1) // 2, d, k],
                device_id=(lax.rem(r + way + rows, rows), c), device_id_type=MESH).wait_recv()

    def start_if(made):
        pl.when(made[0])(made[1].start)

    for k in range(PIECES):
        for d in range(1, min(DIRECT, rows - 1) + 1):
            start_if(col_send_copy(1, d, k))
            start_if(col_send_copy(-1, d, k))
        for d in range(1, pairs):
            row_copy(d, k).start()
        sib_copy(k).start()
    own = [pltpu.make_async_copy(xt, rowbuf.at[:, pl.ds(pl.multiple_of(c * shard, shard), shard), :], own_sem.at[0]),
           pltpu.make_async_copy(xt, colbuf.at[:, pl.ds(pl.multiple_of(r * shard, shard), shard), :], own_sem.at[1])]
    for copy in own:
        copy.start()

    def pass_on(k):
        for d in range(1, pairs):
            row_copy(d, k).wait_recv()
            fwd_copy(d, k).start()
        for d in range(1, rows):
            for way in (1, -1):
                col_wait(way, d, k)
                if d >= DIRECT and d + 1 < rows:
                    start_if(col_send_copy(way, d + 1, k))

    def rest(k):
        sib_copy(k).wait_recv()
        for d in range(1, pairs):
            fwd_copy(d, k).wait_recv()

    stations = members_ref.shape[1]
    sub_at = lax.broadcasted_iota(jnp.int32, (slots, stations), 0)
    slot_ids = jnp.zeros((slots, stations), jnp.int32)
    for s in range(slots):
        slot_ids = jnp.where(sub_at == s, subs_ref[0, s], slot_ids)
    found = jnp.zeros((slots, stations), f32)
    for m in range(members_ref.shape[0]):
        found = jnp.where(slot_ids == members_ref[m:m + 1, :], 1.0, found)
    member[...] = found
    name = lax.broadcasted_iota(jnp.int32, (stations, width), 0)
    block_id, inside = split(lax.broadcasted_iota(jnp.int32, (stations, width), 1), shard)
    picked = jnp.where(name == (block_id * cols + c) * shard + inside, 1.0, 0.0).astype(bf16)
    col_mask = jnp.dot(found.astype(bf16), picked, preferred_element_type=f32)
    lane = lax.broadcasted_iota(jnp.int32, (slots, span), 1)
    row_mask = member[:, pl.ds(pl.multiple_of(r * span, span), span)]

    def prepare(first, last):
        def one(step, carry):
            for u in range(UNROLL):
                i = step * UNROLL + u
                hit = jnp.sum(jnp.where(lane == i, row_mask, 0.0), axis=1, keepdims=True)
                pmask[i] = (hit * col_mask).astype(bf16)
                ids = lax.broadcasted_iota(jnp.int32, (NBIN, width), 0)
                onehot[step, :, u * width:(u + 1) * width] = jnp.where(
                    ids == bins_ref[pl.ds(i, 1), :], 1.0, 0.0).astype(bf16)
            return carry
        lax.fori_loop(first, last, one, 0)

    def correlate(q):
        def one(f, carry):
            cross[pl.ds(f, span, stride=freqs), :] = lax.dot_general(
                rowbuf[f], colbuf[f], NT, preferred_element_type=f32)
            return carry
        lax.fori_loop(q * half, (q + 1) * half, one, 0, unroll=4)

    def build(q, step, w):
        for u in range(UNROLL):
            i = step * UNROLL + u
            block = cross[pl.ds(pl.multiple_of(i * freqs + q * half, half), half), :].astype(bf16)
            weighted = pmask[i][:, None, :] * block[None]
            w[:, u * width:(u + 1) * width] = weighted.reshape(slots * half, width)

    def multiply(step, w):
        acc[...] += lax.dot_general(w[...], onehot[step], NT, preferred_element_type=f32)

    def accumulate(q, first, last):
        def two(pair, carry):
            build(q, 2 * pair + 1, w1)
            multiply(2 * pair, w0)
            build(q, lax.min(2 * pair + 2, steps - 1), w0)
            multiply(2 * pair + 1, w1)
            return carry
        lax.fori_loop(first, last, two, 0)

    def copy1(q, d):
        to = lax.rem(c + d, cols)
        return pltpu.make_async_remote_copy(
            part.at[q, to], got1.at[q, d], send1.at[q, d], recv1.at[q, d], device_id=(r, to), device_id_type=MESH)

    def hand_out(q):
        for k in range(cols):
            for s in range(slots):
                part[q, k, s * share:(s + 1) * share, :] = acc[s * half + k * share:s * half + (k + 1) * share, :]
        for d in range(1, cols):
            copy1(q, d).start()

    quarter = steps // 4
    per_half = PIECES // HALVES
    prepare(0, quarter * 2)
    pass_on(0)
    prepare(quarter * 2, quarter * 3)
    pass_on(1)
    prepare(quarter * 3, steps)
    for copy in own:
        copy.wait()
    for k in range(per_half):
        rest(k)
    correlate(0)
    acc[...] = jnp.zeros_like(acc)
    build(0, 0, w0)
    accumulate(0, 0, steps // 4)
    pass_on(2)
    accumulate(0, steps // 4, steps // 2)
    hand_out(0)
    pass_on(3)
    for k in range(per_half, PIECES):
        rest(k)
    correlate(1)
    acc[...] = jnp.zeros_like(acc)
    build(1, 0, w0)
    accumulate(1, 0, steps // 2)
    hand_out(1)

    depth = slots * share
    shape = (rows * share * cols, depth)
    rid, tail = split(lax.broadcasted_iota(jnp.int32, shape, 0), share * cols)
    fid, sid = split(tail, cols)
    place, fin = split(lax.broadcasted_iota(jnp.int32, shape, 1), share)
    listed = jnp.zeros(shape, jnp.int32)
    for s in range(slots):
        listed = jnp.where(place == s, subs_ref[0, s], listed)
    chosen = jnp.where((rid * cols + sid == listed) & (fid == fin), 1.0, 0.0)

    def copy2(q, d):
        to = lax.rem(r + d, rows)
        return pltpu.make_async_remote_copy(
            spread.at[q, to], got2.at[q, d], send2.at[q, d], recv2.at[q, d], device_id=(to, c), device_id_type=MESH)

    for q in range(HALVES):
        total = part[q, c]
        for d in range(1, cols):
            copy1(q, d).wait()
            total = total + got1[q, d]
        spread[q] = jnp.dot(chosen, total, precision=lax.Precision.HIGHEST,
                            preferred_element_type=f32).reshape(rows, share * cols, NBIN)
        for d in range(1, rows):
            copy2(q, d).start()
    for q in range(HALVES):
        fetches[q].wait()
        total = spread[q, r]
        for d in range(1, rows):
            copy2(q, d).wait()
            total = total + got2[q, d]
        binned = total.astype(bf16)
        for f in range(share):
            power = jnp.dot(binned[f * cols:(f + 1) * cols], kern[q, f], preferred_element_type=f32)
            power = power * lax.rsqrt(jnp.mean(power * power, axis=1, keepdims=True) + 1e-06)
            for k in range(cols):
                ready[k, q * share + f:q * share + f + 1, :] = power[k:k + 1]

    def copy3(d):
        to = lax.rem(c + d, cols)
        return pltpu.make_async_remote_copy(
            ready.at[to], got3.at[d], send3.at[d], recv3.at[d], device_id=(r, to), device_id_type=MESH)

    def put(source, block):
        for q in range(HALVES):
            for f in range(share):
                out_ref[0, pl.ds(q * half + source * share + f, 1), :] = block[q * share + f:q * share + f + 1]

    for d in range(1, cols):
        copy3(d).start()
    put(c, ready[c])
    for d in range(1, cols):
        copy3(d).wait()
        put(lax.rem(c - d + cols, cols), got3[d])
    for k in range(PIECES):
        sib_copy(k).wait_send()
        for d in range(1, pairs):
            row_copy(d, k).wait_send()
            fwd_copy(d, k).wait_send()
        for d in range(1, rows):
            for way in (1, -1):
                made = col_send_copy(way, d, k)
                pl.when(made[0])(made[1].wait_send)


def on_device(spectra, pair_bins, row_subs, station_subs, kernel):
    shard, freqs, width = spectra.shape
    rows, cols = lax.axis_size("row"), lax.axis_size("col")
    span, group = pair_bins.shape
    slots = row_subs.shape[1]
    half = freqs // HALVES
    share = half // cols
    depth = slots * share
    speeds = kernel.shape[2]
    pairs = cols // 2
    dma = pltpu.SemaphoreType.DMA
    vmem = pl.BlockSpec(memory_space=pltpu.VMEM)
    bf16, f32 = jnp.bfloat16, jnp.float32
    return pl.pallas_call(
        functools.partial(body, rows, cols),
        out_shape=jax.ShapeDtypeStruct((1, freqs, speeds), f32),
        in_specs=[vmem, vmem, pl.BlockSpec(memory_space=pltpu.SMEM), vmem, pl.BlockSpec(memory_space=pl.ANY)],
        out_specs=vmem,
        scratch_shapes=[
            pltpu.VMEM((shard * freqs, width), f32),
            pltpu.VMEM((freqs, shard, width), bf16),
            pltpu.VMEM((freqs, cols * shard, width), bf16),
            pltpu.VMEM((freqs, rows * shard, width), bf16),
            pltpu.VMEM((slots, station_subs.shape[0]), f32),
            pltpu.VMEM((span, slots, group), bf16),
            pltpu.VMEM((span // UNROLL, NBIN, UNROLL * group), bf16),
            pltpu.VMEM((span * freqs, group), f32),
            pltpu.VMEM((slots * half, UNROLL * group), bf16),
            pltpu.VMEM((slots * half, UNROLL * group), bf16),
            pltpu.VMEM((slots * half, NBIN), f32),
            pltpu.VMEM((HALVES, cols, depth, NBIN), f32),
            pltpu.VMEM((HALVES, cols, depth, NBIN), f32),
            pltpu.VMEM((HALVES, rows, share * cols, NBIN), f32),
            pltpu.VMEM((HALVES, rows, share * cols, NBIN), f32),
            pltpu.VMEM((cols, HALVES * share, speeds), f32),
            pltpu.VMEM((cols, HALVES * share, speeds), f32),
            pltpu.VMEM((HALVES, share, NBIN, speeds), bf16),
            dma((2,)), dma((HALVES,)),
            dma((pairs, PIECES)), dma((pairs, PIECES)), dma((PIECES,)), dma((PIECES,)),
            dma((pairs, PIECES)), dma((pairs, PIECES)),
            dma((2, rows, PIECES)), dma((2, rows, PIECES)),
            dma((HALVES, cols)), dma((HALVES, cols)), dma((HALVES, rows)), dma((HALVES, rows)),
            dma((cols,)), dma((cols,)),
        ],
        compiler_params=pltpu.CompilerParams(collective_id=0, has_side_effects=True, vmem_limit_bytes=62 << 20),
        name="dispersion",
    )(spectra, pair_bins, row_subs, station_subs.T, kernel)


def solution(mesh):
    in_specs = (P(("row", "col"), None, None), P("row", "col"), P("row", None), P(), P())
    out_specs = P(("row", "col"), None, None)
    return jax.shard_map(
        on_device, mesh=mesh, in_specs=in_specs, out_specs=out_specs, check_vma=False
    )
```

time: 182 us -> 65.3 us (0.36)
  waiting for transfers between devices: 111 us -> 0 us
  Pallas kernels: 0 us -> 63.8 us
  matrix products: 21.9 us -> 0 us
  local copies, waits for them, and re-layouts: 19 us -> 1.38 us
  between operations: 13.2 us -> 0.01 us
  blocking collectives: 8.21 us -> 0 us
  other arithmetic: 6.36 us -> 0 us
    pallas_call x0 -> x1, Pallas kernels: none -> 63.8 us  [on_device(): pl.pallas_call(functools.partial(body, rows, cols), out_shape=jax.ShapeDt...]
    all_gather x2 -> x0, waiting for transfers between devices: 56.4 us -> none  [the longest x1 29.4 us: on_device(): row_spectra = lax.all_gather(spectra, 'col', axis=0, tiled=True)]
    reduce_scatter x2 -> x0, waiting for transfers between devices: 54.1 us -> none  [the longest x1 34.2 us: on_device(): lax.psum_scatter(partial_value, 'col', scatter_dimension=1, tiled=True)]
    dot_general x19 -> x0, matrix products: 21.9 us -> none  [the longest x16 15.6 us: accumulate(): jnp.dot(weighted.reshape(slot_count * F, step_rows * col_span), onehot, p...]
    eq x16 -> x0, local copies, waits for them, and re-layouts: 11.2 us -> none  [accumulate(): onehot = (bins_part.reshape(-1, 1) == bin_ids[None, :]).astype(jnp.bfloat16)]
    all_to_all x1 -> x0, blocking collectives: 8.21 us -> none  [on_device(): lax.all_to_all(binned, 'col', split_axis=0, concat_axis=1, tiled=True)]
    mul x33 -> x0, other arithmetic: 4.46 us -> none  [the longest x32 3.76 us: accumulate(): mask_part[:, None, :, None] * col_mask[:, None, None, :] * cross_part[None]]
    dynamic_slice x33 -> x0, local copies, waits for them, and re-layouts: 2.46 us -> none  [the longest x16 1.32 us: accumulate(): mask_part = lax.dynamic_slice_in_dim(row_mask, first_row, step_rows, 1)]
  transfers between devices with their start and end apart: 4 -> 0, of which waited for: 4 -> 0; matrix products, arithmetic and copies ran while one was open for 2% -> 0% of each run, Pallas kernels for 0% -> 0%
where the time goes in v2:
time: 65.3 us; the launch traced here: 65.1 us
  Pallas kernels  63.8 us (98%)
  local copies, waits for them, and re-layouts  1.38 us (2%)
    pallas_call x1, Pallas kernels, on_device(): pl.pallas_call(functools.partial(body, rows, cols), out_shape=jax.ShapeDt...  63.8 us
    unnamed x1, local copies, waits for them, and re-layouts  1.38 us

profile of v2, /device:TPU:0, one launch (start us, length us, event | category | flops | bytes accessed | tf_op | source)
XLA Modules:
  0.0 65.1 jit_solution(13742231245528575020)
XLA Ops:
  0.0 63.8 %dispersion.1 = f32[1,32,256]{2,1,0:T(8,128)} custom-call(bf16[32,32,128]{2,1,0:T(8,128)(2,1)} %x_ref.1, s32[256,128]{1,0:T(8,128)} %bins_ref.1, s32[1,16]{1,0:T(1,128)} %subs_ref.1, s32[8,1024]{1,0:T(8,128)} %bitcast.1, bf16[32,256,256]{2,1,0:T(8,128)(2,1)} %kern_ref.1), custom_call_target="tpu_custom_call" | custom-call | tf_op jit(solution)/shard_map/dispersion/pallas_call | solution.py:300
  63.8 1.4 %copy.7 = f32[1,32,256]{2,1,0:T(8,128)} copy(f32[1,32,256]{2,1,0:T(8,128)} %dispersion.1) | data formatting | bytes 65536

commit v3 on v2

--- a/solution.py
+++ b/solution.py
@@ -100,13 +100,17 @@
     def start_if(made):
         pl.when(made[0])(made[1].start)
 
-    for k in range(PIECES):
+    def send(k):
         for d in range(1, min(DIRECT, rows - 1) + 1):
             start_if(col_send_copy(1, d, k))
             start_if(col_send_copy(-1, d, k))
         for d in range(1, pairs):
             row_copy(d, k).start()
         sib_copy(k).start()
+
+    per_half = PIECES // HALVES
+    for k in range(per_half):
+        send(k)
     own = [pltpu.make_async_copy(xt, rowbuf.at[:, pl.ds(pl.multiple_of(c * shard, shard), shard), :], own_sem.at[0]),
            pltpu.make_async_copy(xt, colbuf.at[:, pl.ds(pl.multiple_of(r * shard, shard), shard), :], own_sem.at[1])]
     for copy in own:
@@ -193,12 +197,38 @@
         for d in range(1, cols):
             copy1(q, d).start()
 
+    depth = slots * share
+    shape = (rows * share * cols, depth)
+    rid, tail = split(lax.broadcasted_iota(jnp.int32, shape, 0), share * cols)
+    fid, sid = split(tail, cols)
+    place, fin = split(lax.broadcasted_iota(jnp.int32, shape, 1), share)
+    listed = jnp.zeros(shape, jnp.int32)
+    for s in range(slots):
+        listed = jnp.where(place == s, subs_ref[0, s], listed)
+    chosen = jnp.where((rid * cols + sid == listed) & (fid == fin), 1.0, 0.0)
+
+    def copy2(q, d):
+        to = lax.rem(r + d, rows)
+        return pltpu.make_async_remote_copy(
+            spread.at[q, to], got2.at[q, d], send2.at[q, d], recv2.at[q, d], device_id=(to, c), device_id_type=MESH)
+
+    def to_owners(q):
+        total = part[q, c]
+        for d in range(1, cols):
+            copy1(q, d).wait()
+            total = total + got1[q, d]
+        spread[q] = jnp.dot(chosen, total, precision=lax.Precision.HIGHEST,
+                            preferred_element_type=f32).reshape(rows, share * cols, NBIN)
+        for d in range(1, rows):
+            copy2(q, d).start()
+
     quarter = steps // 4
-    per_half = PIECES // HALVES
     prepare(0, quarter * 2)
     pass_on(0)
+    send(2)
     prepare(quarter * 2, quarter * 3)
     pass_on(1)
+    send(3)
     prepare(quarter * 3, steps)
     for copy in own:
         copy.wait()
@@ -217,33 +247,12 @@
     correlate(1)
     acc[...] = jnp.zeros_like(acc)
     build(1, 0, w0)
-    accumulate(1, 0, steps // 2)
+    accumulate(1, 0, steps // 4)
+    to_owners(0)
+    accumulate(1, steps // 4, steps // 2)
     hand_out(1)
-
-    depth = slots * share
-    shape = (rows * share * cols, depth)
-    rid, tail = split(lax.broadcasted_iota(jnp.int32, shape, 0), share * cols)
-    fid, sid = split(tail, cols)
-    place, fin = split(lax.broadcasted_iota(jnp.int32, shape, 1), share)
-    listed = jnp.zeros(shape, jnp.int32)
-    for s in range(slots):
-        listed = jnp.where(place == s, subs_ref[0, s], listed)
-    chosen = jnp.where((rid * cols + sid == listed) & (fid == fin), 1.0, 0.0)
-
-    def copy2(q, d):
-        to = lax.rem(r + d, rows)
-        return pltpu.make_async_remote_copy(
-            spread.at[q, to], got2.at[q, d], send2.at[q, d], recv2.at[q, d], device_id=(to, c), device_id_type=MESH)
-
-    for q in range(HALVES):
-        total = part[q, c]
-        for d in range(1, cols):
-            copy1(q, d).wait()
-            total = total + got1[q, d]
-        spread[q] = jnp.dot(chosen, total, precision=lax.Precision.HIGHEST,
-                            preferred_element_type=f32).reshape(rows, share * cols, NBIN)
-        for d in range(1, rows):
-            copy2(q, d).start()
+    to_owners(1)
+
     for q in range(HALVES):
         fetches[q].wait()
         total = spread[q, r]

time: 65.3 us -> 66.6 us (1.020)
  Pallas kernels: 63.8 us -> 65 us
    pallas_call x1, Pallas kernels: 63.8 us -> 65 us  [on_device(): pl.pallas_call(functools.partial(body, rows, cols), out_shape=jax.ShapeDt...]
where the time goes in v3:
time: 66.6 us; the launch traced here: 66.4 us
  Pallas kernels  65 us (98%)
  local copies, waits for them, and re-layouts  1.38 us (2%)
    pallas_call x1, Pallas kernels, on_device(): pl.pallas_call(functools.partial(body, rows, cols), out_shape=jax.ShapeDt...  65 us
    unnamed x1, local copies, waits for them, and re-layouts  1.38 us

profile of v3, /device:TPU:0, one launch (start us, length us, event | category | flops | bytes accessed | tf_op | source)
XLA Modules:
  0.0 66.4 jit_solution(5233024693968354005)
XLA Ops:
  0.0 65.0 %dispersion.1 = f32[1,32,256]{2,1,0:T(8,128)} custom-call(bf16[32,32,128]{2,1,0:T(8,128)(2,1)} %x_ref.1, s32[256,128]{1,0:T(8,128)} %bins_ref.1, s32[1,16]{1,0:T(1,128)} %subs_ref.1, s32[8,1024]{1,0:T(8,128)} %bitcast.1, bf16[32,256,256]{2,1,0:T(8,128)(2,1)} %kern_ref.1), custom_call_target="tpu_custom_call" | custom-call | tf_op jit(solution)/shard_map/dispersion/pallas_call | solution.py:309
  65.0 1.4 %copy.7 = f32[1,32,256]{2,1,0:T(8,128)} copy(f32[1,32,256]{2,1,0:T(8,128)} %dispersion.1) | data formatting | bytes 65536

commit v4 on v3

--- a/solution.py
+++ b/solution.py
@@ -38,6 +38,7 @@
     half = freqs // HALVES
     share = half // cols
     steps = span // UNROLL
+    per_half = PIECES // HALVES
     bf16, f32 = jnp.bfloat16, jnp.float32
 
     barrier = pltpu.get_barrier_semaphore()
@@ -69,12 +70,16 @@
             device_id=(r, sib), device_id_type=MESH)
 
     def fwd_copy(d, k):
+        if k >= per_half:
+            return pltpu.make_async_remote_copy(
+                xt.at[pl.ds(k * psize, psize)], slot(rowbuf, c, k), fwd_send.at[d, k], fwd_recv.at[d, k],
+                device_id=(r, lax.rem(g + d, pairs) * 2 + (1 - h)), device_id_type=MESH)
         place = slot(rowbuf, lax.rem(g - d + pairs, pairs) * 2 + h, k)
         return pltpu.make_async_remote_copy(
             place, place, fwd_send.at[d, k], fwd_recv.at[d, k], device_id=(r, sib), device_id_type=MESH)
 
     def col_send_copy(way, d, k):
-        if d <= DIRECT:
+        if d <= DIRECT or k >= per_half:
             return (r + way * d >= 0) & (r + way * d < rows), pltpu.make_async_remote_copy(
                 xt.at[pl.ds(k * psize, psize)], slot(colbuf, r, k),
                 col_send.at[(way + 1) // 2, d, k], col_recv.at[(way + 1) // 2, d, k],
@@ -101,14 +106,15 @@
         pl.when(made[0])(made[1].start)
 
     def send(k):
-        for d in range(1, min(DIRECT, rows - 1) + 1):
+        for d in range(1, (min(DIRECT, rows - 1) if k < per_half else rows - 1) + 1):
             start_if(col_send_copy(1, d, k))
             start_if(col_send_copy(-1, d, k))
         for d in range(1, pairs):
             row_copy(d, k).start()
+            if k >= per_half:
+                fwd_copy(d, k).start()
         sib_copy(k).start()
 
-    per_half = PIECES // HALVES
     for k in range(per_half):
         send(k)
     own = [pltpu.make_async_copy(xt, rowbuf.at[:, pl.ds(pl.multiple_of(c * shard, shard), shard), :], own_sem.at[0]),
@@ -120,13 +126,19 @@
         for d in range(1, pairs):
             row_copy(d, k).wait_recv()
             fwd_copy(d, k).start()
-        for d in range(1, rows):
+        for d in range(1, rows - 1):
             for way in (1, -1):
                 col_wait(way, d, k)
-                if d >= DIRECT and d + 1 < rows:
+                if d >= DIRECT:
                     start_if(col_send_copy(way, d + 1, k))
 
     def rest(k):
+        if k >= per_half:
+            for d in range(1, pairs):
+                row_copy(d, k).wait_recv()
+        for d in range(1 if k >= per_half else rows - 1, rows):
+            for way in (1, -1):
+                col_wait(way, d, k)
         sib_copy(k).wait_recv()
         for d in range(1, pairs):
             fwd_copy(d, k).wait_recv()
@@ -222,14 +234,12 @@
         for d in range(1, rows):
             copy2(q, d).start()
 
-    quarter = steps // 4
-    prepare(0, quarter * 2)
-    pass_on(0)
-    send(2)
-    prepare(quarter * 2, quarter * 3)
-    pass_on(1)
-    send(3)
-    prepare(quarter * 3, steps)
+    prepare(0, steps // 2)
+    for k in range(per_half):
+        pass_on(k)
+    for k in range(per_half, PIECES):
+        send(k)
+    prepare(steps // 2, steps)
     for copy in own:
         copy.wait()
     for k in range(per_half):
@@ -237,11 +247,8 @@
     correlate(0)
     acc[...] = jnp.zeros_like(acc)
     build(0, 0, w0)
-    accumulate(0, 0, steps // 4)
-    pass_on(2)
-    accumulate(0, steps // 4, steps // 2)
+    accumulate(0, 0, steps // 2)
     hand_out(0)
-    pass_on(3)
     for k in range(per_half, PIECES):
         rest(k)
     correlate(1)

time: 66.6 us -> 63.5 us (0.953)
  Pallas kernels: 65 us -> 61.9 us
    pallas_call x1, Pallas kernels: 65 us -> 61.9 us  [on_device(): pl.pallas_call(functools.partial(body, rows, cols), out_shape=jax.ShapeDt...]
where the time goes in v4:
time: 63.5 us; the launch traced here: 63.3 us
  Pallas kernels  61.9 us (97%)
  local copies, waits for them, and re-layouts  1.38 us (2%)
    pallas_call x1, Pallas kernels, on_device(): pl.pallas_call(functools.partial(body, rows, cols), out_shape=jax.ShapeDt...  61.9 us
    unnamed x1, local copies, waits for them, and re-layouts  1.38 us

profile of v4, /device:TPU:0, one launch (start us, length us, event | category | flops | bytes accessed | tf_op | source)
XLA Modules:
  0.0 63.3 jit_solution(16211551449947747038)
XLA Ops:
  0.0 61.9 %dispersion.1 = f32[1,32,256]{2,1,0:T(8,128)} custom-call(bf16[32,32,128]{2,1,0:T(8,128)(2,1)} %x_ref.1, s32[256,128]{1,0:T(8,128)} %bins_ref.1, s32[1,16]{1,0:T(1,128)} %subs_ref.1, s32[8,1024]{1,0:T(8,128)} %bitcast.1, bf16[32,256,256]{2,1,0:T(8,128)(2,1)} %kern_ref.1), custom_call_target="tpu_custom_call" | custom-call | tf_op jit(solution)/shard_map/dispersion/pallas_call | solution.py:316
  61.9 1.4 %copy.7 = f32[1,32,256]{2,1,0:T(8,128)} copy(f32[1,32,256]{2,1,0:T(8,128)} %dispersion.1) | data formatting | bytes 65536
